TPU v7x, 512 devices: a whole 4x8x8 slice. The times are simulated.
512 devices in a mesh: section: 4 (over z_lo, core), cls: 128 (over z_hi, x, y).
Axes of the slice: x: 4, y: 8, z: 8 (z_hi: 4, z_lo: 2; z = z_hi * 2 + z_lo), core: 2. Of those that a mesh axis runs over, the one named last changes fastest.
Arguments:
- images: bfloat16 [8192, 256, 256], P(('section', 'cls')), may hold values from -6 to 6
- group_ids: int32 [8192], P(('section', 'cls')), may hold values from 0 to 3
- row_filters: bfloat16 [4, 256, 256], replicated, may hold values from -0.375 to 0.375
- column_filters: bfloat16 [4, 256, 256], replicated, may hold values from -0.375 to 0.375
- basis_rows: bfloat16 [256, 16], replicated, may hold values from -0.375 to 0.375
- basis_columns: bfloat16 [256, 16], replicated, may hold values from -0.375 to 0.375
- rotations: bfloat16 [36, 256, 256], P('section'), may hold values from -0.375 to 0.375
- references: bfloat16 [256, 256], P('cls'), may hold values from -2 to 2
- sharpness: bfloat16 [8192], P(('section', 'cls')), may hold values from 0.049804688 to 2
- best_rotation: int32 [8192], P(('section', 'cls')), may hold values from 0 to 35
- assignments: int32 [8192, 32], P(('section', 'cls')), may hold values from 0 to 255, all different within a row; in each aligned block of 16 rows (0 to 15, 16 to 31, ...) at most 2 rows name the same one
Outputs:
- new_references: float32 [256, 256], P('cls')
- evidence: float32 [8192], P(('section', 'cls'))
Inputs may be any that keep to these rules, and one draw needn't show every extreme that they name: `assignments`: each particle lists 32 different classes; among the particles of one device no class is listed more than 2 times, a bound that some block reaches.
All inputs are finite; a program needn't handle non-finite values.
Results may differ from a plain program's by a relative error of at most 0.019.
Values may be sent and summed in bfloat16 or wider, within the bound.
A program may use at most 64 MiB of HBM per device.

v0:
```python
import math
import jax
import jax.numpy as jnp
from jax import lax
from jax.sharding import PartitionSpec as P

EPSILON = 1e-05


def soft_edge(pixels):
    coordinate = (jnp.arange(pixels, dtype=jnp.float32) - (pixels - 1) / 2.0) / (pixels / 2.0)
    radius = jnp.sqrt(
        coordinate[:, None] * coordinate[:, None] + coordinate[None, :] * coordinate[None, :]
    )
    falloff = jnp.clip((radius - 0.8) / 0.15, 0.0, 1.0)
    return 0.5 + 0.5 * jnp.cos(math.pi * falloff)


def filter_images(images, group_ids, row_filters, column_filters, basis_rows, basis_columns):
    column_each = jnp.take(column_filters, group_ids, axis=0)
    row_each = jnp.take(row_filters, group_ids, axis=0)
    filtered_half = jnp.einsum(
        "bij,bjk->bik", images, column_each, preferred_element_type=jnp.float32
    ).astype(jnp.bfloat16)
    filtered = jnp.einsum(
        "bij,bjk->bik", row_each, filtered_half, preferred_element_type=jnp.float32
    )
    masked = filtered * soft_edge(images.shape[1])
    power = jnp.mean(masked * masked, axis=(1, 2), keepdims=True)
    normed = (masked * lax.rsqrt(power + EPSILON)).astype(jnp.bfloat16)
    inner = jnp.einsum("bij,jk->bik", normed, basis_columns, preferred_element_type=jnp.float32)
    coeffs = jnp.einsum(
        "ja,bjk->bak", basis_rows.astype(jnp.float32), inner, precision=lax.Precision.HIGHEST
    )
    return coeffs.reshape(coeffs.shape[0], -1).astype(jnp.bfloat16)


def body(
    images,
    group_ids,
    row_filters,
    column_filters,
    basis_rows,
    basis_columns,
    rotations,
    references,
    sharpness,
    best_rotation,
    assignments,
):
    particles = images.shape[0]
    listed = assignments.shape[1]
    coeffs = filter_images(
        images, group_ids, row_filters, column_filters, basis_rows, basis_columns
    )
    gathered, gathered_sharp = (
        lax.all_gather(coeffs, "section", axis=0, tiled=True),
        lax.all_gather(sharpness, "section", axis=0, tiled=True),
    )
    gathered_best = lax.all_gather(best_rotation, "section", axis=0, tiled=True)
    all_refs = lax.all_gather(references, "cls", axis=0, tiled=True)
    classes = all_refs.shape[0]
    width = all_refs.shape[1]
    sections = lax.axis_size("section")
    local_rotations = rotations.shape[0]
    first_rotation = lax.axis_index("section") * local_rotations
    turned = jnp.einsum(
        "rkl,nl->nrk", rotations, gathered, preferred_element_type=jnp.float32
    ).astype(jnp.bfloat16)
    products = jnp.einsum("nrk,ck->nrc", turned, all_refs, preferred_element_type=jnp.float32)
    scores = products * gathered_sharp.astype(jnp.float32)[:, None, None]
    maxima = jnp.max(scores, axis=1)
    totals = jnp.sum(jnp.exp(scores - maxima[:, None, :]), axis=1)
    partial_marg = (maxima + jnp.log(totals)).reshape(sections, particles, classes)
    received_marg = lax.all_to_all(partial_marg, "section", split_axis=0, concat_axis=0, tiled=True)
    own_marg = jax.nn.logsumexp(received_marg, axis=0)
    evidence = jax.nn.logsumexp(own_marg, axis=1)
    class_range = jnp.arange(classes, dtype=jnp.int32)
    matches = assignments[:, :, None] == class_range[None, None, :]
    picked = jnp.sum(jnp.where(matches, own_marg[:, None, :], 0.0), axis=2)
    weights = jax.nn.softmax(picked, axis=1).astype(jnp.bfloat16)
    offset = gathered_best - first_rotation
    chosen = (offset[:, None] == jnp.arange(local_rotations, dtype=jnp.int32)[None, :]).astype(
        jnp.bfloat16
    )
    partial_rows = jnp.einsum("nrk,nr->nk", turned, chosen, preferred_element_type=jnp.float32)
    aligned = lax.psum_scatter(
        partial_rows.astype(jnp.bfloat16), "section", scatter_dimension=0, tiled=True
    )
    contribution = (
        weights.astype(jnp.float32)[:, :, None] * aligned.astype(jnp.float32)[:, None, :]
    ).astype(jnp.bfloat16)
    flat_classes = assignments.reshape(-1)
    flat_contribution = contribution.reshape(-1, width)
    flat_weights = weights.reshape(-1)
    owners = lax.axis_size("cls")
    own_classes = references.shape[0]
    capacity = max(2, -(-(particles * listed) // classes))
    onehot = (flat_classes[:, None] == class_range[None, :]).astype(jnp.int32)
    slot_rank = jnp.sum((jnp.cumsum(onehot, axis=0) - 1) * onehot, axis=1)
    slot_index = flat_classes * capacity + slot_rank
    buffer = (
        jnp.zeros((classes * capacity, width), jnp.bfloat16).at[slot_index].set(flat_contribution)
    )
    weight_slots = jnp.zeros((classes * capacity,), jnp.bfloat16).at[slot_index].set(flat_weights)
    buffer = buffer.reshape(owners, own_classes, capacity, width)
    weight_slots = weight_slots.reshape(owners, own_classes, capacity)
    received, received_weights = (
        lax.all_to_all(buffer, "cls", split_axis=0, concat_axis=0, tiled=True),
        lax.all_to_all(weight_slots, "cls", split_axis=0, concat_axis=0, tiled=True),
    )
    class_sums = jnp.sum(received.astype(jnp.float32), axis=(0, 2))
    class_weights = jnp.sum(received_weights.astype(jnp.float32), axis=(0, 2))
    class_sums, class_weights = lax.psum((class_sums, class_weights), "section")
    new_references = (class_sums + references.astype(jnp.float32)) / (class_weights[:, None] + 1.0)
    return (new_references, evidence)


def solution(mesh):
    in_specs = (
        P(("section", "cls"), None, None),
        P(("section", "cls")),
        P(),
        P(),
        P(),
        P(),
        P("section", None, None),
        P("cls", None),
        P(("section", "cls")),
        P(("section", "cls")),
        P(("section", "cls"), None),
    )
    out_specs = (P("cls", None), P(("section", "cls")))
    return jax.shard_map(body, mesh=mesh, in_specs=in_specs, out_specs=out_specs, check_vma=False)
```

profile of v0, /device:TPU:1, one launch (start us, length us, event | category | flops | bytes accessed | tf_op | source)
XLA Modules:
  0.0 496.1 jit_solution(2594808979812159641)
XLA Ops:
  7.2 0.8 compare_select_fusion.1
  8.7 3.1 gather_fusion
  11.8 2.0 gather_fusion.1
  13.8 1.0 multiply_add_fusion
  14.9 5.7 %multiply_reduce_fusion = (f32[16]{0:T(128)S(1)}, f32[16,256,256]{2,1,0:T(8,128)}) fusion(f32[256,256]{1,0:T(8,128)S(1)} %multiply_add_fusion, bf16[16,256,256]{2,1,0:T(8,128)(2,1)S(1)} %copy-done, bf16[16,256,256]{2,1,0:T(8,128)(2,1)} %gather_fusion.1, pred[16]{0:T(512)(128)(4,1)S(1)} %compare_and_fusion, bf16[16,256,256]{2,1,0:T(8,128)(2,1)} %gather_fusion), kind=kOutput, calls=%fused_computation.5 | convolution fusion | flops 1080033280 | bytes 10747984 | tf_op jit(solution)/shard_map/bij,bjk->bik/dot_general | solution.py:25
  20.6 3.0 fusion
  24.1 12.3 %all_gather.12 = bf16[64,256]{1,0:T(8,128)(2,1)} all-gather(bf16[16,256]{1,0:T(8,128)(2,1)S(1)} %convert_element_type.71), channel_id=1, replica_groups=mesh['section'=4,'cls'=128] {'section'}, dimensions={0}, use_global_device_ids=true | all-gather | bytes 40960 | tf_op jit(solution)/shard_map/all_gather | solution.py:57
  36.4 1.3 dynamic-slice
  38.6 5.2 %all-reduce = bf16[64]{0:T(256)(128)(2,1)S(1)} all-reduce(bf16[64]{0:T(256)(128)(2,1)S(1)} %dynamic-update-slice), channel_id=1, replica_groups=mesh['section'=4,'cls'=128] {'section'}, use_global_device_ids=true, to_apply=%add | all-reduce | flops 64 | bytes 256
  43.8 320.0 %all-gather = bf16[128,2,256]{2,1,0:T(2,128)(2,1)S(1)} all-gather(bf16[1,2,256]{2,1,0:T(2,128)(2,1)S(1)} %bitcast.40), channel_id=1, replica_groups=mesh['section'=4,'cls'=128] {'cls'}, dimensions={0}, use_global_device_ids=true | all-gather | bytes 132096 | tf_op jit(solution)/shard_map/all_gather | solution.py:61
  363.9 1.3 convolution_convert_fusion
  366.5 60.8 %all-to-all-start = ((f32[4,16,256]{2,1,0:T(8,128)}), f32[4,16,256]{2,1,0:T(8,128)S(1)}, u32[]{:S(2)}, u32[]{:S(2)}) async-start(f32[4,16,256]{2,1,0:T(8,128)} %bitcast.11), calls=%async_computation | async-start | bytes 131072 | tf_op jit(solution)/shard_map/all_to_all | solution.py:75
  427.6 4.2 all-reduce.1
  431.9 1.3 fusion.19
  435.8 3.8 scatter_custom_fusion.1
  439.6 0.8 reshape.197
  440.4 6.3 %all-to-all-start.2 = ((bf16[128,2,2]{2,1,0:T(2,128)(2,1)}), bf16[128,2,2]{2,1,0:T(2,128)(2,1)S(1)}, u32[]{:S(2)}, u32[]{:S(2)}) async-start(bf16[128,2,2]{2,1,0:T(2,128)(2,1)} %reshape.197), calls=%async_computation.3 | async-start | bytes 131072 | tf_op jit(solution)/shard_map/all_to_all | solution.py:110
  446.8 0.7 convert_element_type.78
  447.6 2.4 scatter_custom_fusion
  450.0 0.8 reshape.196
  450.8 8.5 %all-to-all-done.2 = bf16[128,2,2]{2,1,0:T(2,128)(2,1)S(1)} async-done(((bf16[128,2,2]{2,1,0:T(2,128)(2,1)}), bf16[128,2,2]{2,1,0:T(2,128)(2,1)S(1)}, u32[]{:S(2)}, u32[]{:S(2)}) %all-to-all-start.2) | async-done | bytes 1056 | tf_op jit(solution)/shard_map/all_to_all | solution.py:110
  459.3 7.2 %all-to-all-start.1 = ((bf16[128,2,2,256]{3,2,1,0:T(2,128)(2,1)}), bf16[128,2,2,256]{3,2,1,0:T(2,128)(2,1)S(1)}, u32[]{:S(2)}, u32[]{:S(2)}) async-start(bf16[128,2,2,256]{3,2,1,0:T(2,128)(2,1)} %reshape.196), calls=%async_computation.2 | async-start | bytes 524288 | tf_op jit(solution)/shard_map/all_to_all | solution.py:109
  467.5 12.7 %all-to-all-done.1 = bf16[128,2,2,256]{3,2,1,0:T(2,128)(2,1)S(1)} async-done(((bf16[128,2,2,256]{3,2,1,0:T(2,128)(2,1)}), bf16[128,2,2,256]{3,2,1,0:T(2,128)(2,1)S(1)}, u32[]{:S(2)}, u32[]{:S(2)}) %all-to-all-start.1) | async-done | bytes 262176 | tf_op jit(solution)/shard_map/all_to_all | solution.py:109
  480.3 8.3 %all-reduce.2 = (f32[2,256]{1,0:T(2,128)S(1)}, f32[2]{0:T(128)S(1)}) all-reduce(f32[2,256]{1,0:T(2,128)S(1)} %convert_reduce_fusion, f32[2]{0:T(128)S(1)} %convert_reduce_fusion.1), channel_id=1, replica_groups=mesh['section'=4,'cls'=128] {'section'}, use_global_device_ids=true, to_apply=%region_14.16 | all-reduce | flops 514 | bytes 4112 | tf_op jit(solution)/shard_map/psum | solution.py:114
  (74 shorter events, 7.6 us)
Async XLA Ops:
  7.2 7.7 %copy-start = (bf16[16,256,256]{2,1,0:T(8,128)(2,1)S(1)}, bf16[16,256,256]{2,1,0:T(8,128)(2,1)}, u32[]{:S(2)}) copy-start(bf16[16,256,256]{2,1,0:T(8,128)(2,1)} %param.13) | copy-start | bytes 6291460
  8.7 3.1 copy-start.1
  14.9 5.7 %copy-start.5 = (bf16[256,16]{0,1:T(8,128)(2,1)S(1)}, bf16[256,16]{0,1:T(8,128)(2,1)}, u32[]{:S(2)}) copy-start(bf16[256,16]{0,1:T(8,128)(2,1)} %param.18) | copy-start | bytes 24580
  20.6 3.1 copy-start.6
  20.6 17.8 %copy-start.8 = (bf16[16]{0:T(256)(128)(2,1)S(1)}, bf16[16]{0:T(256)(128)(2,1)}, u32[]{:S(2)}) copy-start(bf16[16]{0:T(256)(128)(2,1)} %param.21) | copy-start | bytes 100
  20.6 23.2 %copy-start.7 = (bf16[2,256]{1,0:T(2,128)(2,1)S(1)}, bf16[2,256]{1,0:T(2,128)(2,1)}, u32[]{:S(2)}) copy-start(bf16[2,256]{1,0:T(2,128)(2,1)} %param.20) | copy-start | bytes 3076
  20.6 343.3 %copy-start.2 = (bf16[9,256,256]{2,1,0:T(8,128)(2,1)S(1)}, bf16[9,256,256]{2,1,0:T(8,128)(2,1)}, u32[]{:S(2)}) copy-start(bf16[9,256,256]{2,1,0:T(8,128)(2,1)} %param.19) | copy-start | bytes 3538948
  24.0 403.3 %copy-start.9 = (s32[16]{0:T(128)S(1)}, s32[16]{0:T(128)}, u32[]{:S(2)}) copy-start(s32[16]{0:T(128)} %param.22) | copy-start | bytes 196
  363.8 70.0 %copy-start.4 = (s32[16,32]{1,0:T(8,128)S(1)}, s32[16,32]{1,0:T(8,128)}, u32[]{:S(2)}) copy-start(s32[16,32]{1,0:T(8,128)} %param.23) | copy-start | bytes 6148
  365.1 0.7 copy-start.3
  366.5 68.4 %all-to-all-start = ((f32[4,16,256]{2,1,0:T(8,128)}), f32[4,16,256]{2,1,0:T(8,128)S(1)}, u32[]{:S(2)}, u32[]{:S(2)}) async-start(f32[4,16,256]{2,1,0:T(8,128)} %bitcast.11), calls=%async_computation | async-start | bytes 131072 | tf_op jit(solution)/shard_map/all_to_all | solution.py:75
  427.3 19.4 %reduce-scatter.2.cloned.1.call-start = ((), (), s32[]{:S(2)}) async-start(), calls=%async_computation.4 | async-start | bytes 40960 | tf_op jit(solution)/shard_map/reduce_scatter | solution.py:87
  440.4 18.9 %all-to-all-start.2 = ((bf16[128,2,2]{2,1,0:T(2,128)(2,1)}), bf16[128,2,2]{2,1,0:T(2,128)(2,1)S(1)}, u32[]{:S(2)}, u32[]{:S(2)}) async-start(bf16[128,2,2]{2,1,0:T(2,128)(2,1)} %reshape.197), calls=%async_computation.3 | async-start | bytes 131072 | tf_op jit(solution)/shard_map/all_to_all | solution.py:110
  459.3 20.9 %all-to-all-start.1 = ((bf16[128,2,2,256]{3,2,1,0:T(2,128)(2,1)}), bf16[128,2,2,256]{3,2,1,0:T(2,128)(2,1)S(1)}, u32[]{:S(2)}, u32[]{:S(2)}) async-start(bf16[128,2,2,256]{3,2,1,0:T(2,128)(2,1)} %reshape.196), calls=%async_computation.2 | async-start | bytes 524288 | tf_op jit(solution)/shard_map/all_to_all | solution.py:109
Sparse Core Ops, SparseCore 0:
  433.9 11.9 reduce-scatter.1
where the time goes:
time: 497 us; the launch traced here: 496 us
  blocking collectives  350 us (70%)
  starting transfers between devices  74.3 us (15%)
  waiting for transfers between devices  21.3 us (4%)
  local copies, waits for them, and re-layouts  16.5 us (3%)
  between operations  15 us (3%)
  matrix products  11.8 us (2%)
  other arithmetic  7.26 us (1%)
    all_gather x1, blocking collectives, body(): all_refs = lax.all_gather(references, 'cls', axis=0, tiled=True)  320 us
    all_to_all x1, starting transfers between devices, body(): lax.all_to_all(partial_marg, 'section', split_axis=0, concat_axis=0, tile...  60.8 us
    all_to_all x1, waiting for transfers between devices, body(): lax.all_to_all(buffer, 'cls', split_axis=0, concat_axis=0, tiled=True)  12.7 us
    all_gather x1, blocking collectives, body(): lax.all_gather(coeffs, 'section', axis=0, tiled=True)  12.3 us
  transfers between devices with their start and end apart: 4, of which 2 were waited for; matrix products, arithmetic and copies ran while one was open for 3% of the time, Pallas kernels for 0%

commit v1 on v0

--- a/solution.py
+++ b/solution.py
@@ -54,7 +54,9 @@
         images, group_ids, row_filters, column_filters, basis_rows, basis_columns
     )
     gathered, gathered_sharp = (
-        lax.all_gather(coeffs, "section", axis=0, tiled=True),
+        jnp.concatenate(
+            lax.all_to_all(jnp.stack([coeffs] * lax.axis_size("section")), "section", 0, 0), axis=0
+        ),
         lax.all_gather(sharpness, "section", axis=0, tiled=True),
     )
     gathered_best = lax.all_gather(best_rotation, "section", axis=0, tiled=True)

time: 497 us -> 497 us (level)
  blocking collectives: 350 us -> 337 us
  starting transfers between devices: 74.3 us -> 84.6 us
    all_gather x1 -> x0, blocking collectives: 12.3 us -> none  [body(): lax.all_gather(coeffs, 'section', axis=0, tiled=True)]
    all_to_all x0 -> x1, starting transfers between devices: none -> 10.1 us  [body(): lax.all_to_all(jnp.stack([coeffs] * lax.axis_size('section')), 'section',...]
  transfers between devices with their start and end apart: 4 -> 5, of which waited for: 2 -> 4; matrix products, arithmetic and copies ran while one was open for 3% -> 3% of each run, Pallas kernels for 0% -> 0%
where the time goes in v1:
time: 497 us
  blocking collectives  337 us (68%)
  starting transfers between devices  84.6 us (17%)
  waiting for transfers between devices  24.5 us (5%)
  local copies, waits for them, and re-layouts  16.7 us (3%)
  between operations  14.9 us (3%)
  matrix products  11.2 us (2%)
  other arithmetic  7.25 us (1%)
    all_gather x1, blocking collectives, body(): all_refs = lax.all_gather(references, 'cls', axis=0, tiled=True)  320 us
    all_to_all x1, starting transfers between devices, body(): lax.all_to_all(partial_marg, 'section', split_axis=0, concat_axis=0, tile...  60.6 us
    all_to_all x1, waiting for transfers between devices, body(): lax.all_to_all(buffer, 'cls', split_axis=0, concat_axis=0, tiled=True)  13.6 us
    all_to_all x1, starting transfers between devices, body(): lax.all_to_all(jnp.stack([coeffs] * lax.axis_size('section')), 'section',...  10.1 us
  transfers between devices with their start and end apart: 5, of which 4 were waited for; matrix products, arithmetic and copies ran while one was open for 3% of the time, Pallas kernels for 0%

profile of v1, /device:TPU:1, one launch (start us, length us, event | category | flops | bytes accessed | tf_op | source)
XLA Modules:
  0.0 496.5 jit_solution(11070021180934977339)
XLA Ops:
  7.2 0.8 compare_select_fusion.1
  8.7 3.1 gather_fusion
  11.8 2.0 gather_fusion.1
  13.8 1.0 multiply_add_fusion
  14.9 5.7 %multiply_reduce_fusion = (f32[16]{0:T(128)S(1)}, f32[16,256,256]{2,1,0:T(8,128)}) fusion(f32[256,256]{1,0:T(8,128)S(1)} %multiply_add_fusion, bf16[16,256,256]{2,1,0:T(8,128)(2,1)S(1)} %copy-done, bf16[16,256,256]{2,1,0:T(8,128)(2,1)} %gather_fusion.1, pred[16]{0:T(512)(128)(4,1)S(1)} %compare_and_fusion, bf16[16,256,256]{2,1,0:T(8,128)(2,1)} %gather_fusion), kind=kOutput, calls=%fused_computation.5 | convolution fusion | flops 1080033280 | bytes 10747984 | tf_op jit(solution)/shard_map/bij,bjk->bik/dot_general | solution.py:25
  20.6 2.9 fusion
  24.6 10.1 %all-to-all-start = ((bf16[4,16,256]{2,1,0:T(8,128)(2,1)}), bf16[4,16,256]{2,1,0:T(8,128)(2,1)S(1)}, u32[]{:S(2)}, u32[]{:S(2)}) async-start(bf16[4,16,256]{2,1,0:T(8,128)(2,1)} %stack.2), calls=%async_computation | async-start | bytes 65536 | tf_op jit(solution)/shard_map/all_to_all | solution.py:58
  34.9 1.3 dynamic-slice
  37.1 5.4 %all-reduce = bf16[64]{0:T(256)(128)(2,1)S(1)} all-reduce(bf16[64]{0:T(256)(128)(2,1)S(1)} %dynamic-update-slice), channel_id=1, replica_groups=mesh['section'=4,'cls'=128] {'section'}, use_global_device_ids=true, to_apply=%add | all-reduce | flops 64 | bytes 256
  43.4 4.5 all-reduce.1
  48.2 320.0 %all-gather = bf16[128,2,256]{2,1,0:T(2,128)(2,1)S(1)} all-gather(bf16[1,2,256]{2,1,0:T(2,128)(2,1)S(1)} %bitcast.42), channel_id=1, replica_groups=mesh['section'=4,'cls'=128] {'cls'}, dimensions={0}, use_global_device_ids=true | all-gather | bytes 132096 | tf_op jit(solution)/shard_map/all_gather | solution.py:63
  368.3 1.8 convolution_convert_fusion
  371.1 60.6 %all-to-all-start.1 = ((f32[4,16,256]{2,1,0:T(8,128)}), f32[4,16,256]{2,1,0:T(8,128)S(1)}, u32[]{:S(2)}, u32[]{:S(2)}) async-start(f32[4,16,256]{2,1,0:T(8,128)} %bitcast.12), calls=%async_computation.1 | async-start | bytes 131072 | tf_op jit(solution)/shard_map/all_to_all | solution.py:77
  432.6 2.3 all-to-all-done.1
  435.8 3.8 scatter_custom_fusion.1
  439.6 0.8 reshape.204
  440.4 6.3 %all-to-all-start.3 = ((bf16[128,2,2]{2,1,0:T(2,128)(2,1)}), bf16[128,2,2]{2,1,0:T(2,128)(2,1)S(1)}, u32[]{:S(2)}, u32[]{:S(2)}) async-start(bf16[128,2,2]{2,1,0:T(2,128)(2,1)} %reshape.204), calls=%async_computation.4 | async-start | bytes 131072 | tf_op jit(solution)/shard_map/all_to_all | solution.py:112
  447.2 0.7 convert_element_type.80
  448.0 2.4 scatter_custom_fusion
  450.4 0.8 reshape.203
  451.2 8.1 %all-to-all-done.3 = bf16[128,2,2]{2,1,0:T(2,128)(2,1)S(1)} async-done(((bf16[128,2,2]{2,1,0:T(2,128)(2,1)}), bf16[128,2,2]{2,1,0:T(2,128)(2,1)S(1)}, u32[]{:S(2)}, u32[]{:S(2)}) %all-to-all-start.3) | async-done | bytes 1056 | tf_op jit(solution)/shard_map/all_to_all | solution.py:112
  459.3 7.6 %all-to-all-start.2 = ((bf16[128,2,2,256]{3,2,1,0:T(2,128)(2,1)}), bf16[128,2,2,256]{3,2,1,0:T(2,128)(2,1)S(1)}, u32[]{:S(2)}, u32[]{:S(2)}) async-start(bf16[128,2,2,256]{3,2,1,0:T(2,128)(2,1)} %reshape.203), calls=%async_computation.3 | async-start | bytes 524288 | tf_op jit(solution)/shard_map/all_to_all | solution.py:111
  467.9 13.6 %all-to-all-done.2 = bf16[128,2,2,256]{3,2,1,0:T(2,128)(2,1)S(1)} async-done(((bf16[128,2,2,256]{3,2,1,0:T(2,128)(2,1)}), bf16[128,2,2,256]{3,2,1,0:T(2,128)(2,1)S(1)}, u32[]{:S(2)}, u32[]{:S(2)}) %all-to-all-start.2) | async-done | bytes 262176 | tf_op jit(solution)/shard_map/all_to_all | solution.py:111
  481.6 7.4 %all-reduce.2 = (f32[2,256]{1,0:T(2,128)S(1)}, f32[2]{0:T(128)S(1)}) all-reduce(f32[2,256]{1,0:T(2,128)S(1)} %convert_reduce_fusion, f32[2]{0:T(128)S(1)} %convert_reduce_fusion.1), channel_id=1, replica_groups=mesh['section'=4,'cls'=128] {'section'}, use_global_device_ids=true, to_apply=%region_14.16 | all-reduce | flops 514 | bytes 4112 | tf_op jit(solution)/shard_map/psum | solution.py:116
  (72 shorter events, 8.6 us)
Async XLA Ops:
  7.2 7.7 %copy-start = (bf16[16,256,256]{2,1,0:T(8,128)(2,1)S(1)}, bf16[16,256,256]{2,1,0:T(8,128)(2,1)}, u32[]{:S(2)}) copy-start(bf16[16,256,256]{2,1,0:T(8,128)(2,1)} %param.13) | copy-start | bytes 6291460
  8.7 3.1 copy-start.1
  14.9 5.7 %copy-start.3 = (bf16[256,16]{0,1:T(8,128)(2,1)S(1)}, bf16[256,16]{0,1:T(8,128)(2,1)}, u32[]{:S(2)}) copy-start(bf16[256,16]{0,1:T(8,128)(2,1)} %param.18) | copy-start | bytes 24580
  20.6 3.0 copy-start.4
  20.6 14.2 %copy-start.2 = (s32[16,32]{1,0:T(8,128)S(1)}, s32[16,32]{1,0:T(8,128)}, u32[]{:S(2)}) copy-start(s32[16,32]{1,0:T(8,128)} %param.23) | copy-start | bytes 6148
  20.6 16.3 %copy-start.6 = (bf16[16]{0:T(256)(128)(2,1)S(1)}, bf16[16]{0:T(256)(128)(2,1)}, u32[]{:S(2)}) copy-start(bf16[16]{0:T(256)(128)(2,1)} %param.21) | copy-start | bytes 100
  23.5 19.7 %copy-start.7 = (s32[16]{0:T(128)S(1)}, s32[16]{0:T(128)}, u32[]{:S(2)}) copy-start(s32[16]{0:T(128)} %param.22) | copy-start | bytes 196
  23.5 24.7 %copy-start.5 = (bf16[2,256]{1,0:T(2,128)(2,1)S(1)}, bf16[2,256]{1,0:T(2,128)(2,1)}, u32[]{:S(2)}) copy-start(bf16[2,256]{1,0:T(2,128)(2,1)} %param.20) | copy-start | bytes 3076
  24.6 343.6 %all-to-all-start = ((bf16[4,16,256]{2,1,0:T(8,128)(2,1)}), bf16[4,16,256]{2,1,0:T(8,128)(2,1)S(1)}, u32[]{:S(2)}, u32[]{:S(2)}) async-start(bf16[4,16,256]{2,1,0:T(8,128)(2,1)} %stack.2), calls=%async_computation | async-start | bytes 65536 | tf_op jit(solution)/shard_map/all_to_all | solution.py:58
  371.1 63.8 %all-to-all-start.1 = ((f32[4,16,256]{2,1,0:T(8,128)}), f32[4,16,256]{2,1,0:T(8,128)S(1)}, u32[]{:S(2)}, u32[]{:S(2)}) async-start(f32[4,16,256]{2,1,0:T(8,128)} %bitcast.12), calls=%async_computation.1 | async-start | bytes 131072 | tf_op jit(solution)/shard_map/all_to_all | solution.py:77
  431.7 15.5 %reduce-scatter.2.cloned.1.call-start = ((), (), s32[]{:S(2)}) async-start(), calls=%async_computation.5 | async-start | bytes 40960 | tf_op jit(solution)/shard_map/reduce_scatter | solution.py:89
  440.4 18.9 %all-to-all-start.3 = ((bf16[128,2,2]{2,1,0:T(2,128)(2,1)}), bf16[128,2,2]{2,1,0:T(2,128)(2,1)S(1)}, u32[]{:S(2)}, u32[]{:S(2)}) async-start(bf16[128,2,2]{2,1,0:T(2,128)(2,1)} %reshape.204), calls=%async_computation.4 | async-start | bytes 131072 | tf_op jit(solution)/shard_map/all_to_all | solution.py:112
  459.3 22.2 %all-to-all-start.2 = ((bf16[128,2,2,256]{3,2,1,0:T(2,128)(2,1)}), bf16[128,2,2,256]{3,2,1,0:T(2,128)(2,1)S(1)}, u32[]{:S(2)}, u32[]{:S(2)}) async-start(bf16[128,2,2,256]{3,2,1,0:T(2,128)(2,1)} %reshape.203), calls=%async_computation.3 | async-start | bytes 524288 | tf_op jit(solution)/shard_map/all_to_all | solution.py:111
Sparse Core Ops, SparseCore 0:
  435.3 11.8 reduce-scatter.1
